TPU v7x, 32 devices: a whole 2x2x4 slice. The times are simulated.
32 devices in a mesh: clip: 2 (over y), row: 16 (over z, x, core).
Axes of the slice: x: 2, y: 2, z: 4, core: 2. Of those that a mesh axis runs over, the one named last changes fastest.
Arguments:
- features: bfloat16 [1, 64, 48, 384], P(None, ('clip', 'row')), parts along dimension 1, may hold values from -19 to 19
- conv_cache: bfloat16 [2, 64, 48, 384], P(None, ('clip', 'row')), parts along dimension 1, may hold values from -6 to 6
- norm_gain: float32 [384], replicated, may hold values from 0.1 to 1.9
- w_query: bfloat16 [384, 384], replicated
- w_key: bfloat16 [384, 384], replicated
- w_value: bfloat16 [384, 384], replicated, may hold values from -0.3125 to 0.3125
- w_out: bfloat16 [384, 384], replicated
- conv_gain: float32 [384], replicated, may hold values from 0.1 to 1.9
- conv_weight: bfloat16 [3, 3, 3, 384, 384], replicated, may hold values from -0.0625 to 0.0625
Outputs:
- residual_out: float32 [1, 64, 48, 384], P(None, ('clip', 'row')), parts along dimension 1
- conv_out: bfloat16 [1, 64, 48, 384], P(None, ('clip', 'row')), parts along dimension 1
There are 2 independent parts, one for each index of `clip`. A program takes and returns all parts, laid end to end along the dimension named above; an argument that names none is the same for every part. Nothing has to cross between parts.
All inputs are finite; a program needn't handle non-finite values.
Results may differ from a plain program's by a relative error of at most 0.0096.
Values may be sent and summed in bfloat16 or wider, within the bound.
A program may use at most 128 MiB of HBM per device.

v0:
```python
import jax
import jax.numpy as jnp
from jax import lax
from jax.sharding import PartitionSpec as P


def extended_2(block, sides, width):
    for axis, dim in sides:
        count = lax.axis_size(axis)
        forward = [(i, i + 1) for i in range(count - 1)]
        backward = [(target, source) for source, target in forward]
        low = lax.ppermute(
            lax.slice_in_dim(block, block.shape[dim] - width, None, axis=dim), axis, forward
        )
        high = lax.ppermute(lax.slice_in_dim(block, 0, width, axis=dim), axis, backward)
        block = jnp.concatenate([low, block, high], axis=dim)
    return block


def rms_norm(values, gain):
    return values * lax.rsqrt(jnp.mean(values * values, axis=-1, keepdims=True) + 1e-06) * gain


def frame_update(
    running_max, running_sum, running_acc, queries, keys_block, values_block, score_scale
):
    scores = jnp.dot(queries, keys_block.T, preferred_element_type=jnp.float32) * score_scale
    new_max = jnp.maximum(running_max, jnp.max(scores, axis=-1))
    rescale = jnp.exp(running_max - new_max)
    expw = jnp.exp(scores - new_max[:, None])
    new_sum = running_sum * rescale + jnp.sum(expw, axis=-1)
    new_acc = running_acc * rescale[:, None] + jnp.dot(
        expw.astype(jnp.bfloat16), values_block, preferred_element_type=jnp.float32
    )
    return (new_max, new_sum, new_acc)


def shards(features, conv_cache, norm_gain, w_query, w_key, w_value, w_out, conv_gain, conv_weight):
    frame_count, row_count, width_cells, channels = features.shape
    score_scale = channels ** (-0.5)
    query_rows = features.shape[1]
    source = features.astype(jnp.float32)
    normed = rms_norm(source, norm_gain).astype(jnp.bfloat16)
    query_count = query_rows * width_cells
    queries = (
        jnp.dot(normed.reshape(-1, channels), w_query, preferred_element_type=jnp.float32)
        .astype(jnp.bfloat16)
        .reshape(frame_count, query_count, channels)
    )
    start_state = (
        jnp.full((frame_count, query_count), -1e30, jnp.float32),
        jnp.zeros((frame_count, query_count), jnp.float32),
        jnp.zeros((frame_count, query_count, channels), jnp.float32),
    )

    def per_frame(operands):
        running_max, running_sum, running_acc, frame_queries, frame_piece = operands
        frame_normed = (
            rms_norm(frame_piece.astype(jnp.float32), norm_gain)
            .astype(jnp.bfloat16)
            .reshape(-1, channels)
        )
        keys_block = jnp.dot(frame_normed, w_key, preferred_element_type=jnp.float32).astype(
            jnp.bfloat16
        )
        values_block = jnp.dot(frame_normed, w_value, preferred_element_type=jnp.float32).astype(
            jnp.bfloat16
        )
        return frame_update(
            running_max,
            running_sum,
            running_acc,
            frame_queries,
            keys_block,
            values_block,
            score_scale,
        )

    final_max, final_sum, final_acc = lax.map(
        per_frame,
        (
            start_state[0],
            start_state[1],
            start_state[2],
            queries,
            lax.all_gather(features, "row", axis=1, tiled=True),
        ),
    )
    attended = (final_acc / final_sum[:, :, None]).astype(jnp.bfloat16)
    projected = jnp.dot(attended.reshape(-1, channels), w_out, preferred_element_type=jnp.float32)
    residual_all = source + projected.reshape(frame_count, query_rows, width_cells, channels)
    activated = jax.nn.silu(rms_norm(residual_all, conv_gain)).astype(jnp.bfloat16)
    extended = extended_2(jnp.concatenate([conv_cache, activated], axis=0), (("row", 1),), 1)
    padded = jnp.pad(extended, ((0, 0), (0, 0), (1, 1), (0, 0)))
    windows = []
    for shift_t in range(3):
        for shift_y in range(3):
            for shift_x in range(3):
                windows.append(
                    padded[
                        shift_t : shift_t + frame_count,
                        shift_y : shift_y + row_count,
                        shift_x : shift_x + width_cells,
                    ]
                )
    columns = jnp.concatenate(windows, axis=-1).reshape(-1, 27 * channels)
    summed = jnp.dot(
        columns, conv_weight.reshape(27 * channels, channels), preferred_element_type=jnp.float32
    )
    conv_out = summed.reshape(frame_count, row_count, width_cells, channels).astype(jnp.bfloat16)
    return (residual_all, conv_out)


def solution(mesh):
    placed = (
        P(None, ("clip", "row"), None, None),
        P(None, ("clip", "row"), None, None),
        P(),
        P(),
        P(),
        P(),
        P(),
        P(),
        P(),
    )
    return jax.shard_map(
        shards,
        mesh=mesh,
        in_specs=placed,
        out_specs=(P(None, ("clip", "row"), None, None), P(None, ("clip", "row"), None, None)),
        check_vma=False,
    )
```

profile of v0, /device:TPU:1, one launch (start us, length us, event | category | flops | bytes accessed | tf_op | source)
XLA Modules:
  0.0 78.4 jit_solution(6530330871903309043)
XLA Ops:
  7.2 0.0 copy-start
  7.2 0.0 copy-start.7
  7.2 0.0 all-gather.2.cloned.1.call-start
  7.2 0.7 all-gather.2.cloned.1.call-update
  7.9 1.0 %fusion.24 = f32[2,48]{1,0:T(2,128)S(1)} fusion(bf16[1,2,48,384]{3,2,1,0:T(8,128)(2,1)} %param.9), kind=kLoop, calls=%fused_computation.35 | loop fusion | flops 110496 | bytes 74112 | tf_op jit(solution)/shard_map/reduce_sum | solution.py:21
  8.9 1.0 %fusion.26 = bf16[1,2,48,384]{3,2,1,0:T(8,128)(2,1)S(1)} fusion(bf16[1,2,48,384]{3,2,1,0:T(8,128)(2,1)} %param.9, f32[384]{0:T(512)} %param.11, f32[2,48]{1,0:T(2,128)S(1)} %add_rsqrt_fusion.2), kind=kLoop, calls=%fused_computation.37 | loop fusion | flops 147456 | bytes 149376 | tf_op jit(solution)/shard_map/convert_element_type | solution.py:43
  9.9 1.2 %convolution_convert_fusion.2 = bf16[96,384]{1,0:T(8,128)(2,1)S(1)} fusion(bf16[96,384]{1,0:T(8,128)(2,1)S(1)} %bitcast.41, bf16[384,384]{1,0:T(8,128)(2,1)} %param.12), kind=kOutput, calls=%fused_computation.18 | convolution fusion | flops 28348416 | bytes 442368 | tf_op jit(solution)/shard_map/dot_general | solution.py:46
  11.1 40.1 %all-gather.2.cloned.1.call-done = bf16[1,32,48,384]{3,2,0,1:T(8,128)(2,1)} async-done(((bf16[1,2,48,384]{3,2,0,1:T(8,128)(2,1)}), bf16[1,32,48,384]{3,2,0,1:T(8,128)(2,1)}) %all-gather.2.cloned.1.call-update) | async-done | bytes 1179664 | tf_op jit(solution)/shard_map/all_gather | solution.py:86
  51.2 1.7 %multiply_reduce_fusion = f32[32,48]{1,0:T(8,128)S(1)} fusion(bf16[1,32,48,384]{3,2,0,1:T(8,128)(2,1)} %all-gather.2.cloned.1.call-done), kind=kLoop, calls=%fused_computation.6 | loop fusion | flops 1767936 | bytes 1185792 | tf_op jit(solution)/shard_map/while/body/eval_jaxpr/reduce_sum | solution.py:21
  52.9 0.1 rsqrt.30
  52.9 0.0 copy-done.7
  52.9 0.0 copy-done.2
  52.9 0.3 fusion.1
  53.3 0.0 copy-done
  53.3 0.0 copy-start.8
  53.3 1.3 %fusion.31 = (f32[96]{0:T(128)S(1)}, f32[96,1536]{1,0:T(8,128)S(1)}) fusion(bf16[96,384]{1,0:T(8,128)(2,1)S(1)} %convolution_convert_fusion.2, bf16[1536,384]{1,0:T(8,128)(2,1)S(1)} %fusion.1, bf16[384,384]{1,0:T(8,128)(2,1)S(1)} %copy-done), kind=kOutput, calls=%fused_computation.79 | convolution fusion | flops 567115648 | bytes 2138496 | tf_op jit(solution)/shard_map/while/body/eval_jaxpr/dot_general | solution.py:27
  54.6 0.0 copy-start.4
  54.6 0.0 copy-start.5
  54.6 0.2 fusion.16
  54.9 0.0 copy-start.6
  54.9 0.0 copy-start.1
  54.9 1.2 %fusion.8 = bf16[96,384]{1,0:T(8,128)(2,1)S(1)} fusion(bf16[1536,384]{1,0:T(8,128)(2,1)S(1)} %fusion.1, bf16[384,384]{1,0:T(8,128)(2,1)S(1)} %copy-done.8, f32[96,1536]{1,0:T(8,128)S(1)} %get-tuple-element.23, f32[96]{0:T(128)S(1)} %broadcast_maximum_fusion, f32[96]{0:T(128)S(1)} %get-tuple-element.21, f32[96]{0:T(128)S(1)} %get-tuple-element.20), kind=kOutput, calls=%fused_computation.16 | convolution fusion | flops 567226368 | bytes 2139264 | tf_op jit(solution)/shard_map/while/body/eval_jaxpr/dot_general | solution.py:32
  56.2 0.3 multiply_reduce_fusion.1
  56.4 0.0 copy-start.3
  56.5 0.1 multiply_convert_fusion
  56.7 2.5 %collective-permute-start = (bf16[3,1,48,384]{3,2,1,0:T(8,128)(2,1)S(1)}, bf16[3,1,48,384]{3,2,1,0:T(8,128)(2,1)S(1)}, u32[]{:S(2)}, u32[]{:S(2)}) collective-permute-start(bf16[3,1,48,384]{3,2,1,0:T(8,128)(2,1)S(1)} %get-tuple-element.18), channel_id=1, source_target_pairs={{0,1},{1,2},{2,3},{3,4},{4,5},{5,6},{6,7},{7,8},{8,9},{9,10},{10,1... | collective-permute-start | bytes 331784 | tf_op jit(solution)/shard_map/ppermute | solution.py:12
  59.2 1.9 %collective-permute-start.1 = (bf16[3,1,48,384]{3,2,1,0:T(8,128)(2,1)S(1)}, bf16[3,1,48,384]{3,2,1,0:T(8,128)(2,1)S(1)}, u32[]{:S(2)}, u32[]{:S(2)}) collective-permute-start(bf16[3,1,48,384]{3,2,1,0:T(8,128)(2,1)S(1)} %get-tuple-element.19), channel_id=1, source_target_pairs={{1,0},{2,1},{3,2},{4,3},{5,4},{6,5},{7,6},{8,7},{9,8},{10,9},{11,1... | collective-permute-start | bytes 331784 | tf_op jit(solution)/shard_map/ppermute | solution.py:15
  61.1 0.0 collective-permute-done
  61.1 4.1 %collective-permute-done.1 = bf16[3,1,48,384]{3,2,1,0:T(8,128)(2,1)S(1)} collective-permute-done((bf16[3,1,48,384]{3,2,1,0:T(8,128)(2,1)S(1)}, bf16[3,1,48,384]{3,2,1,0:T(8,128)(2,1)S(1)}, u32[]{:S(2)}, u32[]{:S(2)}) %collective-permute-start.1) | collective-permute-done | bytes 110624 | tf_op jit(solution)/shard_map/ppermute | solution.py:15
  65.2 0.2 select_maximum_fusion
  66.0 0.1 constant_dynamic-update-slice_fusion
  66.2 5.4 %fusion.12 = bf16[1,2,48,384]{3,2,1,0:T(8,128)(2,1)} fusion(bf16[10368,384,1]{1,0,2:T(8,128)(2,1)} %bitcast.39, bf16[1,2,48,10368]{3,2,1,0:T(8,128)(2,1)S(1)} %slice_dynamic-update-slice_fusion), kind=kOutput, calls=%fused_computation.19 | convolution fusion | flops 764448768 | bytes 10027008 | tf_op jit(solution)/shard_map/dot_general | solution.py:107
  (39 shorter events, 0.7 us)
Async XLA Ops:
  7.2 46.1 %copy-start = (bf16[384,384]{1,0:T(8,128)(2,1)S(1)}, bf16[384,384]{1,0:T(8,128)(2,1)}, u32[]{:S(2)}) copy-start(bf16[384,384]{1,0:T(8,128)(2,1)} %param.13) | copy-start | bytes 884740
  7.2 45.8 %copy-start.7 = (f32[384]{0:T(512)S(1)}, f32[384]{0:T(512)}, u32[]{:S(2)}) copy-start(f32[384]{0:T(512)} %param.11) | copy-start | bytes 4612
  7.2 44.0 %all-gather.2.cloned.1.call-start = ((), (), s32[]{:S(2)}) async-start(), calls=%async_computation | async-start | bytes 1253376 | tf_op jit(solution)/shard_map/all_gather | solution.py:86
  51.2 1.8 %copy-start.2 = (bf16[1,32,48,384]{3,2,0,1:T(8,128)(2,1)S(1)}, bf16[1,32,48,384]{3,2,0,1:T(8,128)(2,1)}, u32[]{:S(2)}) copy-start(bf16[1,32,48,384]{3,2,0,1:T(8,128)(2,1)} %all-gather.2.cloned.1.call-done) | copy-start | bytes 3538948
  53.3 1.6 %copy-start.8 = (bf16[384,384]{1,0:T(8,128)(2,1)S(1)}, bf16[384,384]{1,0:T(8,128)(2,1)}, u32[]{:S(2)}) copy-start(bf16[384,384]{1,0:T(8,128)(2,1)} %param.14) | copy-start | bytes 884740
  54.6 1.5 %copy-start.4 = (bf16[1,2,48,384]{3,2,1,0:T(8,128)(2,1)S(1)}, bf16[1,2,48,384]{3,2,1,0:T(8,128)(2,1)}, u32[]{:S(2)}) copy-start(bf16[1,2,48,384]{3,2,1,0:T(8,128)(2,1)} %param.9) | copy-start | bytes 221188
  54.6 1.5 %copy-start.5 = (bf16[384,384]{1,0:T(8,128)(2,1)S(1)}, bf16[384,384]{1,0:T(8,128)(2,1)}, u32[]{:S(2)}) copy-start(bf16[384,384]{1,0:T(8,128)(2,1)} %param.15) | copy-start | bytes 884740
  54.9 1.6 %copy-start.6 = (f32[384]{0:T(512)S(1)}, f32[384]{0:T(512)}, u32[]{:S(2)}) copy-start(f32[384]{0:T(512)} %param.16) | copy-start | bytes 4612
  54.9 1.7 %copy-start.1 = (bf16[2,2,48,384]{3,2,1,0:T(8,128)(2,1)S(1)}, bf16[2,2,48,384]{3,2,1,0:T(8,128)(2,1)}, u32[]{:S(2)}) copy-start(bf16[2,2,48,384]{3,2,1,0:T(8,128)(2,1)} %param.10) | copy-start | bytes 442372
  56.4 9.5 %copy-start.3 = (f32[1,2,48,384]{3,2,1,0:T(8,128)}, f32[1,2,48,384]{3,2,1,0:T(8,128)S(1)}, u32[]{:S(2)}) copy-start(f32[1,2,48,384]{3,2,1,0:T(8,128)S(1)} %get-tuple-element.33) | copy-start | bytes 442372
  56.7 4.4 %collective-permute-start = (bf16[3,1,48,384]{3,2,1,0:T(8,128)(2,1)S(1)}, bf16[3,1,48,384]{3,2,1,0:T(8,128)(2,1)S(1)}, u32[]{:S(2)}, u32[]{:S(2)}) collective-permute-start(bf16[3,1,48,384]{3,2,1,0:T(8,128)(2,1)S(1)} %get-tuple-element.18), channel_id=1, source_target_pairs={{0,1},{1,2},{2,3},{3,4},{4,5},{5,6},{6,7},{7,8},{8,9},{9,10},{10,1... | collective-permute-start | bytes 331784 | tf_op jit(solution)/shard_map/ppermute | solution.py:12
  59.2 6.1 %collective-permute-start.1 = (bf16[3,1,48,384]{3,2,1,0:T(8,128)(2,1)S(1)}, bf16[3,1,48,384]{3,2,1,0:T(8,128)(2,1)S(1)}, u32[]{:S(2)}, u32[]{:S(2)}) collective-permute-start(bf16[3,1,48,384]{3,2,1,0:T(8,128)(2,1)S(1)} %get-tuple-element.19), channel_id=1, source_target_pairs={{1,0},{2,1},{3,2},{4,3},{5,4},{6,5},{7,6},{8,7},{9,8},{10,9},{11,1... | collective-permute-start | bytes 331784 | tf_op jit(solution)/shard_map/ppermute | solution.py:15
Sparse Core Ops, SparseCore 0:
  10.3 40.8 all-gather.1
where the time goes:
time: 78.8 us; the launch traced here: 78.4 us
  waiting for transfers between devices  44.9 us (57%)
  between operations  14.4 us (18%)
  matrix products  9.31 us (12%)
  other arithmetic  4.78 us (6%)
  starting transfers between devices  4.46 us (6%)
    all_gather x1, waiting for transfers between devices, shards(): lax.all_gather(features, 'row', axis=1, tiled=True)  40.1 us
    dot_general x1, matrix products, shards(): jnp.dot(columns, conv_weight.reshape(27 * channels, channels), preferred_...  5.38 us
    ppermute x1, waiting for transfers between devices, extended_2(): lax.ppermute(lax.slice_in_dim(block, 0, width, axis=dim), axis, backward)  4.13 us
    reduce_sum x2, other arithmetic, rms_norm(): jnp.mean(values * values, axis=-1, keepdims=True) + 1e-06  2.64 us
    ppermute x1, starting transfers between devices, extended_2(): lax.ppermute(lax.slice_in_dim(block, block.shape[dim] - width, None, axis...  2.5 us
    ppermute x1, starting transfers between devices, extended_2(): lax.ppermute(lax.slice_in_dim(block, 0, width, axis=dim), axis, backward)  1.92 us
  transfers between devices with their start and end apart: 3, of which 2 were waited for; matrix products, arithmetic and copies ran while one was open for 4% of the time, Pallas kernels for 0%

commit v1 on v0

v1 whole, which is shorter than its diff:
```python
import functools
import math

import jax
import jax.numpy as jnp
from jax import lax
from jax.experimental import pallas as pl
from jax.experimental.pallas import tpu as pltpu
from jax.sharding import PartitionSpec as P

MESH = pl.DeviceIdType.MESH
F32 = jnp.float32
BF16 = jnp.bfloat16
INNER = 4
UNROLL = 4


def _rms(v, gain):
    return v * lax.rsqrt(jnp.mean(v * v, axis=-1, keepdims=True) + 1e-06) * gain


def _flip(index, bits):
    bit = 1
    while bit <= bits:
        if bits & bit:
            index = index + bit - 2 * bit * ((index // bit) % 2)
        bit *= 2
    return index


def _when(cond):
    if isinstance(cond, bool):
        return (lambda f: f()) if cond else (lambda f: None)
    return pl.when(cond)


def _both(a, b):
    if isinstance(a, bool) and isinstance(b, bool):
        return a and b
    return jnp.logical_and(a, b)


def kernel(
    count,
    width,
    feat_hbm,
    cache_hbm,
    ng_ref,
    wq_hbm,
    wk_hbm,
    wv_hbm,
    wo_hbm,
    cg_ref,
    cw_hbm,
    res_ref,
    out_ref,
    blocks,
    src,
    ext,
    wq,
    wk,
    wv,
    wo,
    cw,
    qs,
    m_ref,
    l_ref,
    acc,
    cacc,
    load_sem,
    cw_sem,
    halo_send,
    halo_recv,
    z_send,
    x_send,
    c_send,
    recv,
):
    outer = count // INNER
    tokens, channels = feat_hbm.shape
    total = tokens + 2 * width
    me = lax.axis_index("row")
    z = me // INNER
    xpeer = me - z * INNER
    pair = (xpeer // 2) % 2
    core = xpeer % 2
    xpeer = me + 2 - 4 * pair
    cpeer = me + 1 - 2 * core
    static = outer <= UNROLL

    def zpeer(step):
        if static:
            return _flip(z, step)
        return lax.rem(z + step, outer)

    def zfrom(step):
        if static:
            return _flip(z, step)
        return lax.rem(z - step + outer, outer)

    def loop(low, high, body):
        if static:
            for step in range(low, high):
                body(step)
        else:
            lax.fori_loop(low, high, lambda i, carry: (body(i), carry)[1], 0)

    has_prev = me > 0
    has_next = me < count - 1
    prev = jnp.maximum(me - 1, 0)
    after = jnp.minimum(me + 1, count - 1)

    own = pl.ds(width, tokens)
    loads = [
        pltpu.make_async_copy(feat_hbm, src.at[own], load_sem.at[0]),
        pltpu.make_async_copy(wq_hbm, wq, load_sem.at[1]),
        pltpu.make_async_copy(wk_hbm, wk, load_sem.at[2]),
        pltpu.make_async_copy(cache_hbm, ext.at[:, own], load_sem.at[3]),
        pltpu.make_async_copy(wv_hbm, wv, load_sem.at[4]),
        pltpu.make_async_copy(wo_hbm, wo, load_sem.at[5]),
    ]
    wloads = [pltpu.make_async_copy(cw_hbm.at[t], cw.at[t], cw_sem.at[t]) for t in range(3)]
    for copy in loads[:4]:
        copy.start()
    for copy in wloads[:2]:
        copy.start()
    for copy in loads[4:]:
        copy.start()
    wloads[2].start()

    barrier = pltpu.get_barrier_semaphore()

    def greet(device):
        pl.semaphore_signal(barrier, inc=1, device_id={"row": device}, device_id_type=MESH)

    def greet_z(step):
        greet(zpeer(step) * INNER + 2 * pair + core)

    loop(1, outer, greet_z)
    greet(xpeer)
    greet(cpeer)

    greet(lax.rem(me + 1, count))
    greet(lax.rem(me + count - 1, count))
    pl.semaphore_wait(barrier, outer + 3)

    def halo(a, b, index, device):
        return pltpu.make_async_remote_copy(
            src_ref=a,
            dst_ref=b,
            send_sem=halo_send.at[index],
            recv_sem=halo_recv.at[index],
            device_id={"row": device},
            device_id_type=MESH,
        )

    first = pl.ds(0, width)
    last = pl.ds(tokens - width, width)
    low = pl.ds(0, width)
    high = pl.ds(width + tokens, width)
    up_f = halo(feat_hbm.at[last], src.at[low], 0, after)
    down_f = halo(feat_hbm.at[first], src.at[high], 1, prev)
    up_c = halo(cache_hbm.at[:, last], ext.at[:, low], 2, after)
    down_c = halo(cache_hbm.at[:, first], ext.at[:, high], 3, prev)

    @pl.when(has_next)
    def _():
        up_f.start()

    @pl.when(has_prev)
    def _():
        down_f.start()

    def put(ident, sem, device):
        return pltpu.make_async_remote_copy(
            src_ref=blocks.at[ident],
            dst_ref=blocks.at[ident],
            send_sem=sem,
            recv_sem=recv.at[ident],
            device_id={"row": device},
            device_id_type=MESH,
        )

    def at(zi, p, c):
        return zi * INNER + 2 * p + c

    def z_put(step):
        return put(me, z_send.at[step], at(zpeer(step), pair, core))

    def x_put(step):
        return put(at(zfrom(step), pair, core), x_send.at[step], xpeer)

    def c_put(step, which):
        p = pair if which == 0 else 1 - pair
        return put(at(zfrom(step), p, core), c_send.at[which, step], cpeer)

    def arrived(ident):
        put(ident, z_send.at[0], cpeer).wait_recv()

    gain = ng_ref[...].reshape(1, channels)
    loads[0].wait()
    blocks[me] = _rms(src[own, :].astype(F32), gain).astype(BF16)
    loop(1, outer, lambda s: z_put(s).start())
    x_put(0).start()
    c_put(0, 0).start()

    @pl.when(has_next)
    def _():
        up_c.start()

    @pl.when(has_prev)
    def _():
        down_c.start()

    zero = jnp.zeros((width, channels), BF16)

    @pl.when(has_prev)
    def _():
        up_f.wait_recv()

    @pl.when(jnp.logical_not(has_prev))
    def _():
        src[low, :] = zero
        for t in range(ext.shape[0]):
            ext[t, low, :] = zero

    @pl.when(has_next)
    def _():
        down_f.wait_recv()

    @pl.when(jnp.logical_not(has_next))
    def _():
        src[high, :] = zero
        for t in range(ext.shape[0]):
            ext[t, high, :] = zero

    loads[1].wait()
    loads[2].wait()
    normed = _rms(src[...].astype(F32), gain).astype(BF16)
    query = jnp.dot(normed, wq[...], preferred_element_type=F32).astype(BF16)
    folded = lax.dot_general(
        query, wk[...], (((1,), (1,)), ((), ())), preferred_element_type=F32
    )
    qs[...] = (folded * (channels**-0.5 * math.log2(math.e))).astype(BF16)
    m_ref[...] = jnp.full(m_ref.shape, -1e30, F32)
    l_ref[...] = jnp.zeros(l_ref.shape, F32)
    acc[...] = jnp.zeros(acc.shape, F32)

    def conv(frame, t):
        taps = jnp.concatenate(
            [frame[dy * width : dy * width + tokens] for dy in range(3)], axis=-1
        )
        for dx in range(3):
            part = jnp.dot(
                taps,
                cw[t, :, dx].reshape(3 * channels, channels),
                preferred_element_type=F32,
            )
            if t == 0:
                cacc[dx] = part
            else:
                cacc[dx] += part

    def attend(step):
        zi = zfrom(step)
        keys = blocks[pl.ds(zi * INNER, INNER)].reshape(INNER * tokens, channels)
        scores = lax.dot_general(
            qs[...], keys, (((1,), (1,)), ((), ())), preferred_element_type=F32
        )
        old = m_ref[...]
        new = jnp.maximum(old, jnp.max(scores, axis=-1, keepdims=True))
        scale = jnp.exp2(old - new)
        expw = jnp.exp2(scores - new)
        m_ref[...] = new
        l_ref[...] = l_ref[...] * scale + jnp.sum(expw, axis=-1, keepdims=True)
        acc[...] = acc[...] * scale + jnp.dot(
            expw.astype(BF16), keys, preferred_element_type=F32
        )

    def stage_z(step):
        arrived(at(zfrom(step), pair, core))
        x_put(step).start()
        c_put(step, 0).start()

    def stage_x(step):
        arrived(at(zfrom(step), 1 - pair, core))
        c_put(step, 1).start()

    def stage_c(step):
        zi = zfrom(step)
        arrived(at(zi, pair, 1 - core))
        arrived(at(zi, 1 - pair, 1 - core))
        attend(step)

    stage_x(0)
    loads[3].wait()

    @pl.when(has_prev)
    def _():
        up_c.wait_recv()

    @pl.when(has_next)
    def _():
        down_c.wait_recv()

    if static:
        for step in range(1, outer + 2):
            if step < outer:
                stage_z(step)
            if 0 < step - 1 < outer:
                stage_x(step - 1)
            if step <= 2:
                wloads[step - 1].wait()
                conv(ext[step - 1], step - 1)
            if 0 <= step - 2 < outer:
                stage_c(step - 2)
    else:
        for t in range(2):
            wloads[t].wait()
            conv(ext[t], t)
        stage_z(1)

        def body(step):
            stage_z(step)
            stage_x(step - 1)
            stage_c(step - 2)

        loop(2, outer, body)
        stage_x(outer - 1)
        stage_c(outer - 2)
        stage_c(outer - 1)

    loads[4].wait()
    loads[5].wait()
    mixed = (acc[...] / l_ref[...]).astype(BF16)
    attended = jnp.dot(mixed, wv[...], preferred_element_type=F32).astype(BF16)
    residual = src[...].astype(F32) + jnp.dot(attended, wo[...], preferred_element_type=F32)
    res_ref[...] = residual[width : width + tokens]
    v = _rms(residual, cg_ref[...].reshape(1, channels))
    activated = v / (1.0 + jnp.exp(-v))
    spot = lax.broadcasted_iota(jnp.int32, (total, 1), 0)
    start = jnp.where(has_prev, 0, width)
    stop = jnp.where(has_next, total, total - width)
    activated = jnp.where((spot >= start) & (spot < stop), activated, 0.0).astype(BF16)
    wloads[2].wait()
    conv(activated, 2)
    column = lax.broadcasted_iota(jnp.int32, (tokens, 1), 0) % width
    left = jnp.where(column == 0, 0.0, pltpu.roll(cacc[0], 1, 0))
    right = jnp.where(column == width - 1, 0.0, pltpu.roll(cacc[2], tokens - 1, 0))
    out_ref[...] = (left + cacc[1] + right).astype(BF16)

    loop(1, outer, lambda s: z_put(s).wait_send())
    loop(0, outer, lambda s: x_put(s).wait_send())
    loop(0, outer, lambda s: c_put(s, 0).wait_send())
    loop(0, outer, lambda s: c_put(s, 1).wait_send())

    @pl.when(has_next)
    def _():
        up_f.wait_send()
        up_c.wait_send()

    @pl.when(has_prev)
    def _():
        down_f.wait_send()
        down_c.wait_send()


def shards(features, conv_cache, norm_gain, w_query, w_key, w_value, w_out, conv_gain, conv_weight):
    frames, rows, width, channels = features.shape
    cached = conv_cache.shape[0]
    tokens = rows * width
    total = tokens + 2 * width
    count = lax.axis_size("row")
    outer = count // INNER
    hbm = pl.BlockSpec(memory_space=pl.ANY)
    vmem = pl.BlockSpec(memory_space=pltpu.VMEM)
    dma = pltpu.SemaphoreType.DMA
    square = pltpu.VMEM((channels, channels), BF16)
    residual, conv_out = pl.pallas_call(
        functools.partial(kernel, count, width),
        out_shape=(
            jax.ShapeDtypeStruct((tokens, channels), F32),
            jax.ShapeDtypeStruct((tokens, channels), BF16),
        ),
        in_specs=[hbm, hbm, vmem, hbm, hbm, hbm, hbm, vmem, hbm],
        out_specs=(vmem, vmem),
        scratch_shapes=[
            pltpu.VMEM((count, tokens, channels), BF16),
            pltpu.VMEM((total, channels), BF16),
            pltpu.VMEM((cached, total, channels), BF16),
            square,
            square,
            square,
            square,
            pltpu.VMEM(conv_weight.shape, BF16),
            pltpu.VMEM((total, channels), BF16),
            pltpu.VMEM((total, 1), F32),
            pltpu.VMEM((total, 1), F32),
            pltpu.VMEM((total, channels), F32),
            pltpu.VMEM((3, tokens, channels), F32),
            dma((6,)),
            dma((3,)),
            dma((4,)),
            dma((4,)),
            dma((outer,)),
            dma((outer,)),
            dma((2, outer)),
            dma((count,)),
        ],
        compiler_params=pltpu.CompilerParams(
            collective_id=0, has_side_effects=True, vmem_limit_bytes=48 << 20
        ),
    )(
        features.reshape(tokens, channels),
        conv_cache.reshape(cached, tokens, channels),
        norm_gain,
        w_query,
        w_key,
        w_value,
        w_out,
        conv_gain,
        conv_weight,
    )
    return (
        residual.reshape(frames, rows, width, channels),
        conv_out.reshape(frames, rows, width, channels),
    )


def solution(mesh):
    placed = (
        P(None, ("clip", "row"), None, None),
        P(None, ("clip", "row"), None, None),
        P(),
        P(),
        P(),
        P(),
        P(),
        P(),
        P(),
    )
    return jax.shard_map(
        shards,
        mesh=mesh,
        in_specs=placed,
        out_specs=(P(None, ("clip", "row"), None, None), P(None, ("clip", "row"), None, None)),
        check_vma=False,
    )
```

time: 78.8 us -> 33.4 us (0.42)
  the two profiles are of different devices: /device:TPU:1 before, /device:TPU:21 now
where the time goes in v1:
time: 33.4 us; the launch traced here: 33 us
  Pallas kernels  24.1 us (72%)
  local copies, waits for them, and re-layouts  8.29 us (25%)
  between operations  0.66 us (2%)
    pallas_call x1, Pallas kernels, shards(): pl.pallas_call(functools.partial(kernel, count, width), out_shape=(jax.Sh...  24.1 us
    unnamed x18, local copies, waits for them, and re-layouts  8.29 us

profile of v1, /device:TPU:21, one launch (start us, length us, event | category | flops | bytes accessed | tf_op | source)
XLA Modules:
  0.0 33.0 jit_solution(4099523859821824753)
XLA Ops:
  0.6 0.0 copy-start
  0.6 1.0 %copy-done = bf16[384,384]{1,0:T(8,128)(2,1)S(1)} copy-done((bf16[384,384]{1,0:T(8,128)(2,1)S(1)}, bf16[384,384]{1,0:T(8,128)(2,1)}, u32[]{:S(2)}) %copy-start) | copy-done | bytes 294936
  1.6 0.0 copy-start.1
  1.6 1.0 %copy-done.1 = bf16[384,384]{1,0:T(8,128)(2,1)S(1)} copy-done((bf16[384,384]{1,0:T(8,128)(2,1)S(1)}, bf16[384,384]{1,0:T(8,128)(2,1)}, u32[]{:S(2)}) %copy-start.1) | copy-done | bytes 294936
  2.6 0.0 copy-start.2
  2.6 1.0 %copy-done.2 = bf16[384,384]{1,0:T(8,128)(2,1)S(1)} copy-done((bf16[384,384]{1,0:T(8,128)(2,1)S(1)}, bf16[384,384]{1,0:T(8,128)(2,1)}, u32[]{:S(2)}) %copy-start.2) | copy-done | bytes 294936
  3.5 0.0 copy-start.3
  3.5 1.0 %copy-done.3 = bf16[384,384]{1,0:T(8,128)(2,1)S(1)} copy-done((bf16[384,384]{1,0:T(8,128)(2,1)S(1)}, bf16[384,384]{1,0:T(8,128)(2,1)}, u32[]{:S(2)}) %copy-start.3) | copy-done | bytes 294936
  4.5 0.0 copy-start.4
  4.5 0.9 %copy-done.4 = bf16[2,2,48,384]{3,2,1,0:T(8,128)(2,1)S(1)} copy-done((bf16[2,2,48,384]{3,2,1,0:T(8,128)(2,1)S(1)}, bf16[2,2,48,384]{3,2,1,0:T(8,128)(2,1)}, u32[]{:S(2)}) %copy-start.4) | copy-done | bytes 147480
  5.4 0.0 copy-start.5
  5.4 0.9 %copy-done.5 = bf16[1,2,48,384]{3,2,1,0:T(8,128)(2,1)S(1)} copy-done((bf16[1,2,48,384]{3,2,1,0:T(8,128)(2,1)S(1)}, bf16[1,2,48,384]{3,2,1,0:T(8,128)(2,1)}, u32[]{:S(2)}) %copy-start.5) | copy-done | bytes 73752
  6.3 0.0 copy-start.6
  6.3 0.7 %copy-done.6 = f32[384]{0:T(512)S(1)} copy-done((f32[384]{0:T(512)S(1)}, f32[384]{0:T(512)}, u32[]{:S(2)}) %copy-start.6) | copy-done | bytes 1560
  7.0 0.0 copy-start.7
  7.0 0.7 %copy-done.7 = f32[384]{0:T(512)S(1)} copy-done((f32[384]{0:T(512)S(1)}, f32[384]{0:T(512)}, u32[]{:S(2)}) %copy-start.7) | copy-done | bytes 1560
  7.6 24.1 %shard_map.104 = (f32[96,384]{1,0:T(8,128)S(1)}, bf16[96,384]{1,0:T(8,128)(2,1)S(1)}) custom-call(bf16[96,384]{1,0:T(8,128)(2,1)S(1)} %bitcast.6, bf16[2,96,384]{2,1,0:T(8,128)(2,1)S(1)} %bitcast.5, f32[384]{0:T(512)S(1)} %copy-done.6, bf16[384,384]{1,0:T(8,128)(2,1)S(1)} %copy-done, bf16[384,384]{1,0:T(8,128)(2,1)S(1)} %copy-done.1, ...), custom_call_target="tpu_custom_call" | custom-call | tf_op jit(solution)/shard_map/pallas_call | solution.py:379
  31.7 0.7 %copy.13 = f32[1,2,48,384]{3,2,1,0:T(8,128)} copy(f32[1,2,48,384]{3,2,1,0:T(8,128)S(1)} %bitcast.4) | data formatting | bytes 294912
  32.4 0.6 %copy.14 = bf16[1,2,48,384]{3,2,1,0:T(8,128)(2,1)} copy(bf16[1,2,48,384]{3,2,1,0:T(8,128)(2,1)S(1)} %bitcast.7) | data formatting | bytes 147456
Async XLA Ops:
  0.6 1.0 %copy-start = (bf16[384,384]{1,0:T(8,128)(2,1)S(1)}, bf16[384,384]{1,0:T(8,128)(2,1)}, u32[]{:S(2)}) copy-start(bf16[384,384]{1,0:T(8,128)(2,1)} %wq_hbm.1) | copy-start | bytes 884740
  1.6 1.0 %copy-start.1 = (bf16[384,384]{1,0:T(8,128)(2,1)S(1)}, bf16[384,384]{1,0:T(8,128)(2,1)}, u32[]{:S(2)}) copy-start(bf16[384,384]{1,0:T(8,128)(2,1)} %wk_hbm.1) | copy-start | bytes 884740
  2.6 1.0 %copy-start.2 = (bf16[384,384]{1,0:T(8,128)(2,1)S(1)}, bf16[384,384]{1,0:T(8,128)(2,1)}, u32[]{:S(2)}) copy-start(bf16[384,384]{1,0:T(8,128)(2,1)} %wv_hbm.1) | copy-start | bytes 884740
  3.5 1.0 %copy-start.3 = (bf16[384,384]{1,0:T(8,128)(2,1)S(1)}, bf16[384,384]{1,0:T(8,128)(2,1)}, u32[]{:S(2)}) copy-start(bf16[384,384]{1,0:T(8,128)(2,1)} %wo_hbm.1) | copy-start | bytes 884740
  4.5 0.9 %copy-start.4 = (bf16[2,2,48,384]{3,2,1,0:T(8,128)(2,1)S(1)}, bf16[2,2,48,384]{3,2,1,0:T(8,128)(2,1)}, u32[]{:S(2)}) copy-start(bf16[2,2,48,384]{3,2,1,0:T(8,128)(2,1)} %param.10) | copy-start | bytes 442372
  5.4 0.9 %copy-start.5 = (bf16[1,2,48,384]{3,2,1,0:T(8,128)(2,1)S(1)}, bf16[1,2,48,384]{3,2,1,0:T(8,128)(2,1)}, u32[]{:S(2)}) copy-start(bf16[1,2,48,384]{3,2,1,0:T(8,128)(2,1)} %param.9) | copy-start | bytes 221188
  6.3 0.7 %copy-start.6 = (f32[384]{0:T(512)S(1)}, f32[384]{0:T(512)}, u32[]{:S(2)}) copy-start(f32[384]{0:T(512)} %ng_ref.1) | copy-start | bytes 4612
  7.0 0.7 %copy-start.7 = (f32[384]{0:T(512)S(1)}, f32[384]{0:T(512)}, u32[]{:S(2)}) copy-start(f32[384]{0:T(512)} %cg_ref.1) | copy-start | bytes 4612

commit v2 on v1

--- a/solution.py
+++ b/solution.py
@@ -45,15 +45,17 @@
     width,
     feat_hbm,
     cache_hbm,
-    ng_ref,
+    ng_hbm,
     wq_hbm,
     wk_hbm,
     wv_hbm,
     wo_hbm,
-    cg_ref,
+    cg_hbm,
     cw_hbm,
     res_ref,
     out_ref,
+    ng_ref,
+    cg_ref,
     blocks,
     src,
     ext,
@@ -118,7 +120,10 @@
         pltpu.make_async_copy(cache_hbm, ext.at[:, own], load_sem.at[3]),
         pltpu.make_async_copy(wv_hbm, wv, load_sem.at[4]),
         pltpu.make_async_copy(wo_hbm, wo, load_sem.at[5]),
+        pltpu.make_async_copy(cg_hbm, cg_ref, load_sem.at[6]),
     ]
+    gains = pltpu.make_async_copy(ng_hbm, ng_ref, load_sem.at[7])
+    gains.start()
     wloads = [pltpu.make_async_copy(cw_hbm.at[t], cw.at[t], cw_sem.at[t]) for t in range(3)]
     for copy in loads[:4]:
         copy.start()
@@ -197,6 +202,7 @@
     def arrived(ident):
         put(ident, z_send.at[0], cpeer).wait_recv()
 
+    gains.wait()
     gain = ng_ref[...].reshape(1, channels)
     loads[0].wait()
     blocks[me] = _rms(src[own, :].astype(F32), gain).astype(BF16)
@@ -332,6 +338,7 @@
 
     loads[4].wait()
     loads[5].wait()
+    loads[6].wait()
     mixed = (acc[...] / l_ref[...]).astype(BF16)
     attended = jnp.dot(mixed, wv[...], preferred_element_type=F32).astype(BF16)
     residual = src[...].astype(F32) + jnp.dot(attended, wo[...], preferred_element_type=F32)
@@ -372,7 +379,7 @@
     total = tokens + 2 * width
     count = lax.axis_size("row")
     outer = count // INNER
-    hbm = pl.BlockSpec(memory_space=pl.ANY)
+    hbm = pl.BlockSpec(memory_space=pltpu.HBM)
     vmem = pl.BlockSpec(memory_space=pltpu.VMEM)
     dma = pltpu.SemaphoreType.DMA
     square = pltpu.VMEM((channels, channels), BF16)
@@ -382,9 +389,11 @@
             jax.ShapeDtypeStruct((tokens, channels), F32),
             jax.ShapeDtypeStruct((tokens, channels), BF16),
         ),
-        in_specs=[hbm, hbm, vmem, hbm, hbm, hbm, hbm, vmem, hbm],
+        in_specs=[hbm] * 9,
         out_specs=(vmem, vmem),
         scratch_shapes=[
+            pltpu.VMEM((channels,), F32),
+            pltpu.VMEM((channels,), F32),
             pltpu.VMEM((count, tokens, channels), BF16),
             pltpu.VMEM((total, channels), BF16),
             pltpu.VMEM((cached, total, channels), BF16),
@@ -398,7 +407,7 @@
             pltpu.VMEM((total, 1), F32),
             pltpu.VMEM((total, channels), F32),
             pltpu.VMEM((3, tokens, channels), F32),
-            dma((6,)),
+            dma((8,)),
             dma((3,)),
             dma((4,)),
             dma((4,)),
@@ -408,7 +417,7 @@
             dma((count,)),
         ],
         compiler_params=pltpu.CompilerParams(
-            collective_id=0, has_side_effects=True, vmem_limit_bytes=48 << 20
+            collective_id=0, has_side_effects=True, vmem_limit_bytes=(64 << 20) - 65536
         ),
     )(
         features.reshape(tokens, channels),

time: 33.4 us -> 28.8 us (0.86)
  the two profiles are of different devices: /device:TPU:21 before, /device:TPU:17 now
where the time goes in v2:
time: 28.8 us; the launch traced here: 28.6 us
  Pallas kernels  24.9 us (86%)
  local copies, waits for them, and re-layouts  3.1 us (11%)
  between operations  0.64 us (2%)
    pallas_call x1, Pallas kernels, shards(): pl.pallas_call(functools.partial(kernel, count, width), out_shape=(jax.Sh...  24.9 us
    unnamed x2, local copies, waits for them, and re-layouts  3.1 us

profile of v2, /device:TPU:17, one launch (start us, length us, event | category | flops | bytes accessed | tf_op | source)
XLA Modules:
  0.0 28.6 jit_solution(6343116709068944920)
XLA Ops:
  0.6 24.9 %shard_map.104 = (f32[96,384]{1,0:T(8,128)}, bf16[96,384]{1,0:T(8,128)(2,1)}) custom-call(bf16[96,384]{1,0:T(8,128)(2,1)} %bitcast.6, bf16[2,96,384]{2,1,0:T(8,128)(2,1)} %bitcast.5, f32[384]{0:T(512)} %ng_hbm.1, bf16[384,384]{1,0:T(8,128)(2,1)} %wq_hbm.1, bf16[384,384]{1,0:T(8,128)(2,1)} %wk_hbm.1, bf16[384,384]{1,0:T(8,128)(2,1)} %wv_hbm.1, ...), custom_call_target="tpu_custom_call" | custom-call | tf_op jit(solution)/shard_map/pallas_call | solution.py:386
  25.5 1.6 %copy.13 = f32[1,2,48,384]{3,2,1,0:T(8,128)} copy(f32[1,2,48,384]{3,2,1,0:T(8,128)} %bitcast.4) | data formatting | bytes 294912
  27.1 1.5 %copy.14 = bf16[1,2,48,384]{3,2,1,0:T(8,128)(2,1)} copy(bf16[1,2,48,384]{3,2,1,0:T(8,128)(2,1)} %bitcast.7) | data formatting | bytes 147456

commit v3 on v2

--- a/solution.py
+++ b/solution.py
@@ -206,7 +206,8 @@
     gain = ng_ref[...].reshape(1, channels)
     loads[0].wait()
     blocks[me] = _rms(src[own, :].astype(F32), gain).astype(BF16)
-    loop(1, outer, lambda s: z_put(s).start())
+    for s in range(1, min(outer, 3)):
+        z_put(s).start()
     x_put(0).start()
     c_put(0, 0).start()
 
@@ -284,6 +285,12 @@
         )
 
     def stage_z(step):
+        z_put(step).wait_send()
+
+        @_when(step + 2 < outer)
+        def _():
+            z_put(step + 2).start()
+
         arrived(at(zfrom(step), pair, core))
         x_put(step).start()
         c_put(step, 0).start()
@@ -356,7 +363,6 @@
     right = jnp.where(column == width - 1, 0.0, pltpu.roll(cacc[2], tokens - 1, 0))
     out_ref[...] = (left + cacc[1] + right).astype(BF16)
 
-    loop(1, outer, lambda s: z_put(s).wait_send())
     loop(0, outer, lambda s: x_put(s).wait_send())
     loop(0, outer, lambda s: c_put(s, 0).wait_send())
     loop(0, outer, lambda s: c_put(s, 1).wait_send())

time: 28.8 us -> 26.6 us (0.924)
  the two profiles are of different devices: /device:TPU:17 before, /device:TPU:1 now
where the time goes in v3:
time: 26.6 us; the launch traced here: 26.3 us
  Pallas kernels  22.5 us (85%)
  local copies, waits for them, and re-layouts  3.1 us (12%)
  between operations  0.64 us (2%)
    pallas_call x1, Pallas kernels, shards(): pl.pallas_call(functools.partial(kernel, count, width), out_shape=(jax.Sh...  22.5 us
    unnamed x2, local copies, waits for them, and re-layouts  3.1 us

profile of v3, /device:TPU:1, one launch (start us, length us, event | category | flops | bytes accessed | tf_op | source)
XLA Modules:
  0.0 26.3 jit_solution(15754501798122416317)
XLA Ops:
  0.6 22.5 %shard_map.104 = (f32[96,384]{1,0:T(8,128)}, bf16[96,384]{1,0:T(8,128)(2,1)}) custom-call(bf16[96,384]{1,0:T(8,128)(2,1)} %bitcast.6, bf16[2,96,384]{2,1,0:T(8,128)(2,1)} %bitcast.5, f32[384]{0:T(512)} %ng_hbm.1, bf16[384,384]{1,0:T(8,128)(2,1)} %wq_hbm.1, bf16[384,384]{1,0:T(8,128)(2,1)} %wk_hbm.1, bf16[384,384]{1,0:T(8,128)(2,1)} %wv_hbm.1, ...), custom_call_target="tpu_custom_call" | custom-call | tf_op jit(solution)/shard_map/pallas_call | solution.py:392
  23.2 1.6 %copy.13 = f32[1,2,48,384]{3,2,1,0:T(8,128)} copy(f32[1,2,48,384]{3,2,1,0:T(8,128)} %bitcast.4) | data formatting | bytes 294912
  24.7 1.5 %copy.14 = bf16[1,2,48,384]{3,2,1,0:T(8,128)(2,1)} copy(bf16[1,2,48,384]{3,2,1,0:T(8,128)(2,1)} %bitcast.7) | data formatting | bytes 147456

commit v4 on v3

--- a/solution.py
+++ b/solution.py
@@ -423,18 +423,23 @@
             dma((count,)),
         ],
         compiler_params=pltpu.CompilerParams(
-            collective_id=0, has_side_effects=True, vmem_limit_bytes=(64 << 20) - 65536
+            collective_id=0, has_side_effects=True, vmem_limit_bytes=48 << 20
         ),
     )(
-        features.reshape(tokens, channels),
-        conv_cache.reshape(cached, tokens, channels),
-        norm_gain,
-        w_query,
-        w_key,
-        w_value,
-        w_out,
-        conv_gain,
-        conv_weight,
+        *(
+            pltpu.with_memory_space_constraint(x, pltpu.HBM)
+            for x in (
+                features.reshape(tokens, channels),
+                conv_cache.reshape(cached, tokens, channels),
+                norm_gain,
+                w_query,
+                w_key,
+                w_value,
+                w_out,
+                conv_gain,
+                conv_weight,
+            )
+        )
     )
     return (
         residual.reshape(frames, rows, width, channels),

time: 26.6 us -> 24.1 us (0.906)
  local copies, waits for them, and re-layouts: 3.1 us -> 1.3 us
  Pallas kernels: 22.5 us -> 21.9 us
    unnamed x2, local copies, waits for them, and re-layouts: 3.1 us -> 1.3 us
    pallas_call x1, Pallas kernels: 22.5 us -> 21.9 us  [shards(): pl.pallas_call(functools.partial(kernel, count, width), out_shape=(jax.Sh...]
where the time goes in v4:
time: 24.1 us; the launch traced here: 23.8 us
  Pallas kernels  21.9 us (91%)
  local copies, waits for them, and re-layouts  1.3 us (5%)
  between operations  0.64 us (3%)
    pallas_call x1, Pallas kernels, shards(): pl.pallas_call(functools.partial(kernel, count, width), out_shape=(jax.Sh...  21.9 us
    unnamed x2, local copies, waits for them, and re-layouts  1.3 us

profile of v4, /device:TPU:1, one launch (start us, length us, event | category | flops | bytes accessed | tf_op | source)
XLA Modules:
  0.0 23.8 jit_solution(10504840305095864748)
XLA Ops:
  0.6 21.9 %shard_map.104 = (f32[96,384]{1,0:T(8,128)S(1)}, bf16[96,384]{1,0:T(8,128)(2,1)S(1)}) custom-call(bf16[96,384]{1,0:T(8,128)(2,1)} %bitcast.7, bf16[2,96,384]{2,1,0:T(8,128)(2,1)} %bitcast.6, f32[384]{0:T(512)} %ng_hbm.1, bf16[384,384]{1,0:T(8,128)(2,1)} %wq_hbm.1, bf16[384,384]{1,0:T(8,128)(2,1)} %wk_hbm.1, bf16[384,384]{1,0:T(8,128)(2,1)} %wv_hbm.1, ...), custom_call_target="tpu_custom_call" | custom-call | tf_op jit(solution)/shard_map/pallas_call | solution.py:392
  22.5 0.7 %copy.13 = f32[1,2,48,384]{3,2,1,0:T(8,128)} copy(f32[1,2,48,384]{3,2,1,0:T(8,128)S(1)} %bitcast.4) | data formatting | bytes 294912
  23.2 0.6 %copy.14 = bf16[1,2,48,384]{3,2,1,0:T(8,128)(2,1)} copy(bf16[1,2,48,384]{3,2,1,0:T(8,128)(2,1)S(1)} %bitcast.5) | data formatting | bytes 147456

commit v5 on v4

--- a/solution.py
+++ b/solution.py
@@ -13,6 +13,8 @@
 BF16 = jnp.bfloat16
 INNER = 4
 UNROLL = 4
+HALVES = 1
+ORDER = (3, 1, 2)
 
 
 def _rms(v, gain):
@@ -88,7 +90,8 @@
     core = xpeer % 2
     xpeer = me + 2 - 4 * pair
     cpeer = me + 1 - 2 * core
-    static = outer <= UNROLL
+    static = outer == UNROLL
+    piece = tokens // HALVES
 
     def zpeer(step):
         if static:
@@ -176,12 +179,13 @@
     def _():
         down_f.start()
 
-    def put(ident, sem, device):
+    def put(ident, h, sem, device):
+        part = blocks.at[ident, pl.ds(h * piece, piece)]
         return pltpu.make_async_remote_copy(
-            src_ref=blocks.at[ident],
-            dst_ref=blocks.at[ident],
+            src_ref=part,
+            dst_ref=part,
             send_sem=sem,
-            recv_sem=recv.at[ident],
+            recv_sem=recv.at[ident, h],
             device_id={"row": device},
             device_id_type=MESH,
         )
@@ -189,27 +193,34 @@
     def at(zi, p, c):
         return zi * INNER + 2 * p + c
 
-    def z_put(step):
-        return put(me, z_send.at[step], at(zpeer(step), pair, core))
-
-    def x_put(step):
-        return put(at(zfrom(step), pair, core), x_send.at[step], xpeer)
-
-    def c_put(step, which):
+    def z_put(step, h):
+        if static and step == 2:
+            return put(at(zpeer(3), pair, core), h, z_send.at[2, h], at(zpeer(1), pair, core))
+        return put(me, h, z_send.at[step, h], at(zpeer(step), pair, core))
+
+    def x_put(step, h):
+        return put(at(zfrom(step), pair, core), h, x_send.at[step, h], xpeer)
+
+    def c_put(step, h, which):
         p = pair if which == 0 else 1 - pair
-        return put(at(zfrom(step), p, core), c_send.at[which, step], cpeer)
-
-    def arrived(ident):
-        put(ident, z_send.at[0], cpeer).wait_recv()
+        return put(at(zfrom(step), p, core), h, c_send.at[which, step, h], cpeer)
+
+    def arrived(ident, h):
+        put(ident, h, z_send.at[0, h], cpeer).wait_recv()
 
     gains.wait()
     gain = ng_ref[...].reshape(1, channels)
     loads[0].wait()
     blocks[me] = _rms(src[own, :].astype(F32), gain).astype(BF16)
-    for s in range(1, min(outer, 3)):
-        z_put(s).start()
-    x_put(0).start()
-    c_put(0, 0).start()
+    opening = [s for s in ORDER if s != 2] if static else range(1, min(outer, 3))
+    for s in opening:
+        for h in range(HALVES):
+            if s == opening[0] or not static:
+                z_put(s, h).start()
+            if s == opening[0]:
+                x_put(0, h).start()
+    for h in range(HALVES):
+        c_put(0, h, 0).start()
 
     @pl.when(has_next)
     def _():
@@ -241,6 +252,9 @@
         for t in range(ext.shape[0]):
             ext[t, high, :] = zero
 
+    if static:
+        z_put(opening[0], 0).wait_send()
+        z_put(opening[1], 0).start()
     loads[1].wait()
     loads[2].wait()
     normed = _rms(src[...].astype(F32), gain).astype(BF16)
@@ -284,28 +298,31 @@
             expw.astype(BF16), keys, preferred_element_type=F32
         )
 
-    def stage_z(step):
-        z_put(step).wait_send()
-
-        @_when(step + 2 < outer)
-        def _():
-            z_put(step + 2).start()
-
-        arrived(at(zfrom(step), pair, core))
-        x_put(step).start()
-        c_put(step, 0).start()
-
-    def stage_x(step):
-        arrived(at(zfrom(step), 1 - pair, core))
-        c_put(step, 1).start()
-
-    def stage_c(step):
+    def stage_z(step, h):
+        if not static:
+            z_put(step, h).wait_send()
+
+            @pl.when(step + 2 < outer)
+            def _():
+                z_put(step + 2, h).start()
+
+        arrived(at(zfrom(step), pair, core), h)
+        if static and step == 3:
+            z_put(2, h).start()
+        x_put(step, h).start()
+        c_put(step, h, 0).start()
+
+    def stage_x(step, h):
+        arrived(at(zfrom(step), 1 - pair, core), h)
+        c_put(step, h, 1).start()
+
+    def stage_c(step, h):
         zi = zfrom(step)
-        arrived(at(zi, pair, 1 - core))
-        arrived(at(zi, 1 - pair, 1 - core))
-        attend(step)
-
-    stage_x(0)
+        arrived(at(zi, pair, 1 - core), h)
+        arrived(at(zi, 1 - pair, 1 - core), h)
+        if h == HALVES - 1:
+            attend(step)
+
     loads[3].wait()
 
     @pl.when(has_prev)
@@ -317,31 +334,42 @@
         down_c.wait_recv()
 
     if static:
-        for step in range(1, outer + 2):
-            if step < outer:
-                stage_z(step)
-            if 0 < step - 1 < outer:
-                stage_x(step - 1)
-            if step <= 2:
-                wloads[step - 1].wait()
-                conv(ext[step - 1], step - 1)
-            if 0 <= step - 2 < outer:
-                stage_c(step - 2)
+        zunits = [(s, h) for s in ORDER for h in range(HALVES)]
+        units = [(0, h) for h in range(HALVES)] + zunits
+        for i in range(len(units) + 1):
+            if i < len(zunits):
+                stage_z(*zunits[i])
+            if i < len(units):
+                stage_x(*units[i])
+            if i < 2:
+                wloads[i].wait()
+                conv(ext[i], i)
+            if i > 0:
+                stage_c(*units[i - 1])
     else:
+        pieces = range(HALVES)
         for t in range(2):
             wloads[t].wait()
             conv(ext[t], t)
-        stage_z(1)
+        for h in pieces:
+            stage_x(0, h)
+        for h in pieces:
+            stage_z(1, h)
 
         def body(step):
-            stage_z(step)
-            stage_x(step - 1)
-            stage_c(step - 2)
+            for h in pieces:
+                stage_z(step, h)
+            for h in pieces:
+                stage_x(step - 1, h)
+            for h in pieces:
+                stage_c(step - 2, h)
 
         loop(2, outer, body)
-        stage_x(outer - 1)
-        stage_c(outer - 2)
-        stage_c(outer - 1)
+        for h in pieces:
+            stage_x(outer - 1, h)
+        for s in (outer - 2, outer - 1):
+            for h in pieces:
+                stage_c(s, h)
 
     loads[4].wait()
     loads[5].wait()
@@ -363,9 +391,13 @@
     right = jnp.where(column == width - 1, 0.0, pltpu.roll(cacc[2], tokens - 1, 0))
     out_ref[...] = (left + cacc[1] + right).astype(BF16)
 
-    loop(0, outer, lambda s: x_put(s).wait_send())
-    loop(0, outer, lambda s: c_put(s, 0).wait_send())
-    loop(0, outer, lambda s: c_put(s, 1).wait_send())
+    for h in range(HALVES):
+        if static:
+            for s in (opening[1], 2):
+                z_put(s, h).wait_send()
+        loop(0, outer, lambda s: x_put(s, h).wait_send())
+        loop(0, outer, lambda s: c_put(s, h, 0).wait_send())
+        loop(0, outer, lambda s: c_put(s, h, 1).wait_send())
 
     @pl.when(has_next)
     def _():
@@ -417,10 +449,10 @@
             dma((3,)),
             dma((4,)),
             dma((4,)),
-            dma((outer,)),
-            dma((outer,)),
-            dma((2, outer)),
-            dma((count,)),
+            dma((outer, HALVES)),
+            dma((outer, HALVES)),
+            dma((2, outer, HALVES)),
+            dma((count, HALVES)),
         ],
         compiler_params=pltpu.CompilerParams(
             collective_id=0, has_side_effects=True, vmem_limit_bytes=48 << 20

time: 24.1 us -> 23.7 us (0.983)
  Pallas kernels: 21.9 us -> 21.6 us
    pallas_call x1, Pallas kernels: 21.9 us -> 21.6 us  [shards(): pl.pallas_call(functools.partial(kernel, count, width), out_shape=(jax.Sh...]
where the time goes in v5:
time: 23.7 us; the launch traced here: 23.5 us
  Pallas kernels  21.6 us (91%)
  local copies, waits for them, and re-layouts  1.3 us (5%)
  between operations  0.64 us (3%)
    pallas_call x1, Pallas kernels, shards(): pl.pallas_call(functools.partial(kernel, count, width), out_shape=(jax.Sh...  21.6 us
    unnamed x2, local copies, waits for them, and re-layouts  1.3 us

profile of v5, /device:TPU:1, one launch (start us, length us, event | category | flops | bytes accessed | tf_op | source)
XLA Modules:
  0.0 23.5 jit_solution(4438631552542736546)
XLA Ops:
  0.6 21.6 %shard_map.104 = (f32[96,384]{1,0:T(8,128)S(1)}, bf16[96,384]{1,0:T(8,128)(2,1)S(1)}) custom-call(bf16[96,384]{1,0:T(8,128)(2,1)} %bitcast.7, bf16[2,96,384]{2,1,0:T(8,128)(2,1)} %bitcast.6, f32[384]{0:T(512)} %ng_hbm.1, bf16[384,384]{1,0:T(8,128)(2,1)} %wq_hbm.1, bf16[384,384]{1,0:T(8,128)(2,1)} %wk_hbm.1, bf16[384,384]{1,0:T(8,128)(2,1)} %wv_hbm.1, ...), custom_call_target="tpu_custom_call" | custom-call | tf_op jit(solution)/shard_map/pallas_call | solution.py:424
  22.2 0.7 %copy.13 = f32[1,2,48,384]{3,2,1,0:T(8,128)} copy(f32[1,2,48,384]{3,2,1,0:T(8,128)S(1)} %bitcast.4) | data formatting | bytes 294912
  22.9 0.6 %copy.14 = bf16[1,2,48,384]{3,2,1,0:T(8,128)(2,1)} copy(bf16[1,2,48,384]{3,2,1,0:T(8,128)(2,1)S(1)} %bitcast.5) | data formatting | bytes 147456
